TPU v7x, 128 devices: a whole 4x4x4 slice. The times are simulated.
128 devices in a mesh: win: 4 (over z_lo, core), chan: 32 (over y, z_hi, x).
Axes of the slice: x: 4, y: 4, z: 4 (z_hi: 2, z_lo: 2; z = z_hi * 2 + z_lo), core: 2. Of those that a mesh axis runs over, the one named last changes fastest.
Arguments:
- traces: bfloat16 [32, 1024, 7680], P('win', 'chan'), may hold values from -6 to 6
- filter_taps: bfloat16 [32], replicated, may hold values from 0.019897461 to 0.14941406
- good_channels: int32 [1024], P('chan'), may hold values 0 or 1
- source_index: int32 [256], replicated, may hold values from 0 to 1023, as said below
Outputs:
- correlations: float32 [256, 1024, 2048], P('win', 'chan')
Inputs may be any that keep to these rules, and one draw needn't show every extreme that they name: `source_index`: 256 distinct channel numbers; channels 0 and 1023 are among them; how many fall in one device's block varies.
All inputs are finite; a program needn't handle non-finite values. No bound on the sum of `good_channels` on one device may be relied on, other than what follows from the above.
Results may differ from a plain program's by a relative error of at most 0.0071.
Values may be sent and summed in bfloat16 or wider, within the bound.
A program may use at most 192 MiB of HBM per device.

v0:
```python
import math
import jax
import jax.numpy as jnp
from jax import lax
from jax.sharding import PartitionSpec as P

L = 7680
F = 512
LAGS = 2048
HALO = 16
SMOOTH = 64
K0 = 31


def turn(bins, steps):
    phase = jnp.mod(bins * steps, L).astype(jnp.float32) * (2.0 * math.pi / L)
    return (jnp.cos(phase), jnp.sin(phase))


def forward_table():
    bins = K0 + jnp.arange(F, dtype=jnp.int32)
    step = 64
    ca, sa = turn(bins[None, :], step * jnp.arange(L // step, dtype=jnp.int32)[:, None])
    cb, sb = turn(bins[None, :], jnp.arange(step, dtype=jnp.int32)[:, None])
    ca, sa, cb, sb = lax.optimization_barrier((ca, sa, cb, sb))
    cosine = ca[:, None] * cb[None] - sa[:, None] * sb[None]
    sine = sa[:, None] * cb[None] + ca[:, None] * sb[None]
    return (cosine.reshape(L, F).astype(jnp.bfloat16), (-sine).reshape(L, F).astype(jnp.bfloat16))


def inverse_table():
    bins = (K0 + jnp.arange(F, dtype=jnp.int32))[:, None]
    step = 128
    ca, sa = turn(bins, step * jnp.arange(LAGS // step, dtype=jnp.int32)[None, :] - LAGS // 2)
    cb, sb = turn(bins, jnp.arange(step, dtype=jnp.int32)[None, :])
    ca, sa, cb, sb = lax.optimization_barrier((ca, sa, cb, sb))
    cosine = ca[:, :, None] * cb[:, None] - sa[:, :, None] * sb[:, None]
    sine = sa[:, :, None] * cb[:, None] + ca[:, :, None] * sb[:, None]
    return (
        cosine.reshape(F, LAGS).astype(jnp.bfloat16),
        (-sine).reshape(F, LAGS).astype(jnp.bfloat16),
    )


def smoothing():
    positions = jnp.arange(F, dtype=jnp.int32)
    near = (jnp.abs(positions[:, None] - positions[None, :]) <= SMOOTH).astype(jnp.float32)
    return near / jnp.sum(near, axis=0, keepdims=True)


def make_band(filter_taps, channel_count):
    kernel = jnp.concatenate(
        [
            -filter_taps[:HALO].astype(jnp.float32),
            jnp.ones((1,), jnp.float32),
            -filter_taps[HALO:].astype(jnp.float32),
        ]
    )
    row_ids = jnp.arange(channel_count, dtype=jnp.int32)[:, None]
    columns = jnp.arange(channel_count + 2 * HALO, dtype=jnp.int32)[None, :]
    offset = columns - row_ids
    choose = offset[:, :, None] == jnp.arange(2 * HALO + 1, dtype=jnp.int32)[None, None, :]
    return jnp.sum(jnp.where(choose, kernel[None, None, :], 0.0), axis=2)


def with_halo(cells, axis, dim, width):
    count = lax.axis_size(axis)
    ends = count - 1
    head = lax.slice_in_dim(cells, 0, width, axis=dim)
    tail = lax.slice_in_dim(cells, cells.shape[dim] - width, cells.shape[dim], axis=dim)
    before = lax.ppermute(tail, axis, [(i, (i + 1) % count) for i in range(ends)])
    after = lax.ppermute(head, axis, [((i + 1) % count, i) for i in range(ends)])
    return jnp.concatenate([before, cells, after], axis=dim)


def per_device(traces, filter_taps, good_channels, source_index):
    windows, channels, length = traces.shape
    groups, blocks = (lax.axis_size("win"), lax.axis_size("chan"))
    sources = source_index.shape[0]
    bins = F // blocks
    everyone = channels * blocks
    good = good_channels.astype(jnp.float32)[None, :, None]
    rows = traces.reshape(windows * channels, length)
    cosine, sine = forward_table()
    dot = lambda a, b: jnp.dot(a, b, preferred_element_type=jnp.float32)
    spectrum = jnp.stack([dot(rows, cosine), dot(rows, sine)], axis=1)
    spectrum = spectrum.reshape(windows, channels, 2 * F) * good
    padded = with_halo(spectrum, "chan", 1, HALO)
    band = make_band(filter_taps, channels)
    filtered = jnp.einsum("cd,wdf->wcf", band, padded, precision=lax.Precision.HIGHEST) * good
    real, imag = (filtered[..., :F], filtered[..., F:])
    magnitude = jnp.sqrt(real * real + imag * imag).reshape(-1, F)
    amplitude = jnp.dot(magnitude, smoothing(), precision=lax.Precision.HIGHEST)
    divisor = amplitude.reshape(real.shape) + 1e-06
    whitened = jnp.stack([real / divisor, imag / divisor], axis=2).astype(jnp.bfloat16)
    split = whitened.reshape(windows, channels, 2, blocks, bins)
    split = jnp.transpose(split, (3, 4, 2, 0, 1)).reshape(blocks, bins * 2, windows * channels)
    mixed = lax.all_to_all(split, "chan", 0, 0, tiled=True)
    mixed = mixed.reshape(blocks, bins * 2 * windows, channels)
    mixed = jnp.transpose(mixed, (1, 0, 2)).reshape(bins * 2 * windows, everyone)
    ids = jnp.arange(everyone, dtype=jnp.int32)
    selector = (ids[:, None] == source_index[None, :]).astype(jnp.bfloat16)
    picked = dot(mixed, selector).astype(jnp.bfloat16)
    share = sources // groups
    picked = picked.reshape(bins * 2 * windows, groups, share)
    picked = jnp.transpose(picked, (1, 0, 2))
    picked = lax.all_to_all(picked, "win", 0, 0, tiled=True)
    picked = picked.reshape(groups, bins, 2, windows, share)
    picked = jnp.transpose(picked, (1, 2, 0, 3, 4)).reshape(bins, groups * windows, 2 * share)
    gathered = lax.all_gather(picked, "chan", axis=0, tiled=True)
    gathered = gathered.reshape(F, 2 * groups * windows, share)
    own = lax.all_gather(whitened, "win", axis=0, tiled=True)
    own = jnp.transpose(own, (3, 2, 0, 1))
    own_real, own_imag = (own[:, 0], own[:, 1])
    left = jnp.concatenate([own_real, own_imag], axis=1)
    right = jnp.concatenate([own_imag, -own_real], axis=1)
    both = jnp.concatenate([left, right], axis=2)
    stacked = jnp.einsum("fks,fkc->fsc", gathered, both, preferred_element_type=jnp.float32)
    stacked = stacked.astype(jnp.bfloat16).reshape(F, share, 2, channels)
    stacked = jnp.transpose(stacked, (1, 3, 2, 0)).reshape(share * channels, 2, F)
    scaling = 1.0 / math.sqrt(F * windows * groups)
    cosine, sine = inverse_table()
    lagged = (dot(stacked[:, 0], cosine) + dot(stacked[:, 1], sine)) * scaling
    return lagged.reshape(share, channels, LAGS)


def solution(mesh):
    placed = (P("win", "chan", None), P(), P("chan"), P())
    return jax.shard_map(
        per_device, mesh=mesh, in_specs=placed, out_specs=P("win", "chan", None), check_vma=False
    )
```

profile of v0, /device:TPU:0, one launch (start us, length us, event | category | flops | bytes accessed | tf_op | source)
XLA Modules:
  0.0 244.9 jit_solution(9256046249764488601)
XLA Ops:
  6.5 0.5 fusion.53
  7.1 1.1 fusion.46
  8.2 4.6 %subtract_convert_fusion = (bf16[120,64,512]{2,1,0:T(8,128)(2,1)S(1)}, bf16[120,64,512]{2,1,0:T(8,128)(2,1)S(1)}) fusion(f32[64,512]{1,0:T(8,128)S(1)} %get-tuple-element.16, f32[120,512]{1,0:T(8,128)S(1)} %get-tuple-element.15, f32[64,512]{1,0:T(8,128)S(1)} %get-tuple-element.14, f32[120,512]{1,0:T(8,128)S(1)} %get-tuple-element.13), kind=kLoop, calls=%fused_computation.2 | loop fusion | flops 35389440 | bytes 16482304 | tf_op jit(solution)/shard_map/convert_element_type | solution.py:28
  12.8 2.2 convolution_bitcast_fusion
  15.1 2.2 convolution_bitcast_fusion.1
  17.4 0.6 copy.31
  18.0 0.9 reshape.176
  18.9 0.2 broadcast_multiply_fusion
  19.1 0.1 fusion.60
  19.2 3.5 %collective-permute-start = (f32[8,16,1024]{2,1,0:T(8,128)S(1)}, f32[8,16,1024]{2,1,0:T(8,128)S(1)}, u32[]{:S(2)}, u32[]{:S(2)}) collective-permute-start(f32[8,16,1024]{2,1,0:T(8,128)S(1)} %get-tuple-element.27), channel_id=1, source_target_pairs={{0,1},{1,2},{2,3},{3,4},{4,5},{5,6},{6,7},{7,8},{8,9},{9,10},{10,1... | collective-permute-start | bytes 1572872 | tf_op jit(solution)/shard_map/ppermute | solution.py:71
  22.8 1.3 collective-permute-start.1
  24.1 0.1 convert_reduce_fusion
  24.3 0.1 pad_maximum_fusion.2
  24.4 0.1 select_reduce_fusion
  24.5 9.4 %collective-permute-done = f32[8,16,1024]{2,1,0:T(8,128)S(1)} collective-permute-done((f32[8,16,1024]{2,1,0:T(8,128)S(1)}, f32[8,16,1024]{2,1,0:T(8,128)S(1)}, u32[]{:S(2)}, u32[]{:S(2)}) %collective-permute-start) | collective-permute-done | bytes 524320 | tf_op jit(solution)/shard_map/ppermute | solution.py:71
  33.9 4.1 %collective-permute-done.1 = f32[8,16,1024]{2,1,0:T(8,128)S(1)} collective-permute-done((f32[8,16,1024]{2,1,0:T(8,128)S(1)}, f32[8,16,1024]{2,1,0:T(8,128)S(1)}, u32[]{:S(2)}, u32[]{:S(2)}) %collective-permute-start.1) | collective-permute-done | bytes 524320 | tf_op jit(solution)/shard_map/ppermute | solution.py:72
  38.1 1.2 fusion.14
  39.3 1.3 divide_convert_fusion.1
  40.6 0.8 pad_maximum_fusion.1
  41.4 0.2 all-gather.3.cloned.1.call-start
  41.7 0.5 copy.32
  42.2 0.5 copy.33
  42.6 0.5 maximum_bitcast_fusion
  43.1 2.4 copy.34
  45.6 1.5 reshape.177
  47.0 25.4 %all_to_all.10 = bf16[32,32,256]{2,1,0:T(8,128)(2,1)S(1)} all-to-all(bf16[32,32,256]{2,1,0:T(8,128)(2,1)S(1)} %reshape.177), channel_id=1, replica_groups=mesh['win'=4,'chan'=32] {'chan'}, dimensions={0} | all-to-all | bytes 1048576 | tf_op jit(solution)/shard_map/all_to_all | solution.py:98
  72.5 0.9 reshape.178
  73.4 0.8 copy.35
  74.2 0.5 convolution_convert_fusion.1
  74.7 9.1 %all_to_all.11 = bf16[4,256,64]{1,2,0:T(8,128)(2,1)S(1)} all-to-all(bf16[4,256,64]{1,2,0:T(8,128)(2,1)S(1)} %bitcast.90), channel_id=1, replica_groups=mesh['win'=4,'chan'=32] {'win'}, dimensions={0} | all-to-all | bytes 262144 | tf_op jit(solution)/shard_map/all_to_all | solution.py:107
  83.8 0.2 copy.36
  84.0 0.8 reshape.182
  84.9 1.1 fusion.34
  86.0 1.1 fusion.38
  87.1 5.5 %negate_convert_fusion.1 = (bf16[512,16,128]{2,1,0:T(8,128)(2,1)S(1)}, bf16[512,16,128]{2,1,0:T(8,128)(2,1)}) fusion(f32[512,128]{1,0:T(8,128)S(1)} %get-tuple-element.20, f32[512,16]{1,0:T(8,128)S(1)} %get-tuple-element.19, f32[512,128]{1,0:T(8,128)S(1)} %get-tuple-element.18, f32[512,16]{1,0:T(8,128)S(1)} %get-tuple-element.17), kind=kLoop, calls=%fused_computation.5 | loop fusion | flops 9437184 | bytes 4784128 | tf_op jit(solution)/shard_map/convert_element_type | solution.py:41
  92.7 1.3 fusion.59
  94.0 1.8 slice_bitcast_fusion.5
  95.8 2.2 maximum_maximum_fusion
  98.0 13.0 %copy.40 = bf16[512,64,64]{2,1,0:T(8,128)(2,1)} copy(bf16[512,64,64]{0,2,1:T(8,128)(2,1)} %maximum_maximum_fusion) | data formatting | bytes 8388608 | tf_op jit(solution)/shard_map/concatenate | solution.py:117
  111.0 59.2 %all-gather.3.cloned.1.call-done = bf16[512,32,128]{2,1,0:T(8,128)(2,1)} async-done(((bf16[16,32,128]{2,1,0:T(8,128)(2,1)}), bf16[512,32,128]{2,1,0:T(8,128)(2,1)}) %all-gather.3.cloned.1.call-update) | async-done | bytes 4194320 | tf_op jit(solution)/shard_map/all_gather | solution.py:110
  170.2 7.6 %copy.38 = bf16[512,32,128]{0,2,1:T(8,128)(2,1)} copy(bf16[512,32,128]{2,1,0:T(8,128)(2,1)} %all-gather.3.cloned.1.call-done) | data formatting | bytes 8388608 | tf_op jit(solution)/shard_map/all_gather | solution.py:110
  177.8 15.6 %copy.39 = bf16[512,64,64]{1,2,0:T(8,128)(2,1)} copy(bf16[512,64,64]{0,2,1:T(8,128)(2,1)} %bitcast.73) | data formatting | bytes 8388608 | tf_op jit(solution)/shard_map/reshape | solution.py:111
  193.4 11.3 %convolution_convert_fusion = bf16[512,64,64]{2,1,0:T(8,128)(2,1)} fusion(bf16[512,64,64]{1,2,0:T(8,128)(2,1)} %copy.39, bf16[512,64,64]{2,1,0:T(8,128)(2,1)} %copy.40), kind=kOutput, calls=%fused_computation.3 | convolution fusion | flops 270532608 | bytes 12582912 | tf_op jit(solution)/shard_map/fks,fkc->fsc/dot_general | solution.py:118
  204.7 9.7 %copy.41 = bf16[512,64,64]{0,2,1:T(8,128)(2,1)} copy(bf16[512,64,64]{2,1,0:T(8,128)(2,1)} %convolution_convert_fusion) | data formatting | bytes 8388608 | tf_op jit(solution)/shard_map/convert_element_type | solution.py:119
  214.4 2.7 %copy.42 = bf16[64,32,2,512]{3,1,0,2:T(8,128)(2,1)S(1)} copy(bf16[64,32,2,512]{3,1,2,0:T(8,128)(2,1)} %bitcast.74) | data formatting | bytes 8388608 | tf_op jit(solution)/shard_map/transpose | solution.py:120
  217.1 0.2 copy-done
  217.3 8.7 %fusion.2 = f32[2048,2048]{1,0:T(8,128)} fusion(bf16[64,8,16,128]{3,2,1,0:T(8,128)(2,1)S(1)} %bitcast.85, bf16[2048,2,512]{2,0,1:T(8,128)(2,1)S(1)} %bitcast.75), kind=kOutput, calls=%fused_computation.9 | convolution fusion | flops 4294967296 | bytes 20971520 | tf_op jit(solution)/shard_map/dot_general | solution.py:85
  226.0 12.0 %add_multiply_fusion = f32[2048,2048]{1,0:T(8,128)} fusion(f32[2048,2048]{1,0:T(8,128)} %fusion.2, bf16[64,8,16,128]{3,2,1,0:T(8,128)(2,1)S(1)} %bitcast.77, bf16[2048,2,512]{2,0,1:T(8,128)(2,1)S(1)} %bitcast.76), kind=kOutput, calls=%fused_computation | convolution fusion | flops 4303355904 | bytes 37748736 | tf_op jit(solution)/shard_map/dot_general | solution.py:85
  (21 shorter events, 0.3 us)
Async XLA Ops:
  6.5 86.1 %all-gather.5.cloned.1.call-start = ((), (), s32[]{:S(2)}) async-start(), calls=%async_computation.3 | async-start | bytes 2621440 | tf_op jit(solution)/shard_map/all_gather | solution.py:112
  8.2 4.7 %copy-start.2 = (bf16[8,32,7680]{2,1,0:T(8,128)(2,1)S(1)}, bf16[8,32,7680]{2,1,0:T(8,128)(2,1)}, u32[]{:S(2)}) copy-start(bf16[8,32,7680]{2,1,0:T(8,128)(2,1)} %param.4) | copy-start | bytes 11796484
  17.3 1.6 copy-start.4
  17.4 6.8 %copy-start.1 = (bf16[32]{0:T(256)(128)(2,1)S(1)}, bf16[32]{0:T(256)(128)(2,1)}, u32[]{:S(2)}) copy-start(bf16[32]{0:T(256)(128)(2,1)} %param.5) | copy-start | bytes 196
  19.2 14.7 %collective-permute-start = (f32[8,16,1024]{2,1,0:T(8,128)S(1)}, f32[8,16,1024]{2,1,0:T(8,128)S(1)}, u32[]{:S(2)}, u32[]{:S(2)}) collective-permute-start(f32[8,16,1024]{2,1,0:T(8,128)S(1)} %get-tuple-element.27), channel_id=1, source_target_pairs={{0,1},{1,2},{2,3},{3,4},{4,5},{5,6},{6,7},{7,8},{8,9},{9,10},{10,1... | collective-permute-start | bytes 1572872 | tf_op jit(solution)/shard_map/ppermute | solution.py:71
  22.8 15.3 %collective-permute-start.1 = (f32[8,16,1024]{2,1,0:T(8,128)S(1)}, f32[8,16,1024]{2,1,0:T(8,128)S(1)}, u32[]{:S(2)}, u32[]{:S(2)}) collective-permute-start(f32[8,16,1024]{2,1,0:T(8,128)S(1)} %get-tuple-element.28), channel_id=1, source_target_pairs={{1,0},{2,1},{3,2},{4,3},{5,4},{6,5},{7,6},{8,7},{9,8},{10,9},{11,1... | collective-permute-start | bytes 1572872 | tf_op jit(solution)/shard_map/ppermute | solution.py:72
  41.4 128.8 %all-gather.3.cloned.1.call-start = ((), (), s32[]{:S(2)}) async-start(), calls=%async_computation.2 | async-start | bytes 4325376 | tf_op jit(solution)/shard_map/all_gather | solution.py:110
  45.6 28.6 %copy-start.3 = (s32[256]{0:T(256)S(1)}, s32[256]{0:T(256)}, u32[]{:S(2)}) copy-start(s32[256]{0:T(256)} %param.7) | copy-start | bytes 3076
  214.4 2.9 %copy-start = (bf16[512,16,128]{2,1,0:T(8,128)(2,1)S(1)}, bf16[512,16,128]{2,1,0:T(8,128)(2,1)}, u32[]{:S(2)}) copy-start(bf16[512,16,128]{2,1,0:T(8,128)(2,1)} %get-tuple-element.26) | copy-start | bytes 6291460
Sparse Core Ops, SparseCore 0:
  41.6 41.6 all-gather.4
  86.2 83.9 all-gather.2
where the time goes:
time: 246 us; the launch traced here: 245 us
  waiting for transfers between devices  72.8 us (30%)
  local copies, waits for them, and re-layouts  59.7 us (24%)
  matrix products  39.6 us (16%)
  blocking collectives  34.5 us (14%)
  other arithmetic  19.5 us (8%)
  between operations  13.7 us (6%)
  starting transfers between devices  5.06 us (2%)
    all_gather x1, waiting for transfers between devices, per_device(): gathered = lax.all_gather(picked, 'chan', axis=0, tiled=True)  59.2 us
    dot_general x5, matrix products, per_device(): dot = lambda a, b: jnp.dot(a, b, preferred_element_type=jnp.float32)  25.7 us
    all_to_all x1, blocking collectives, per_device(): mixed = lax.all_to_all(split, 'chan', 0, 0, tiled=True)  25.4 us
    reshape x1, local copies, waits for them, and re-layouts, per_device(): gathered = gathered.reshape(F, 2 * groups * windows, share)  15.6 us
    concatenate x1, local copies, waits for them, and re-layouts, per_device(): both = jnp.concatenate([left, right], axis=2)  13 us
    dot_general x1, matrix products, per_device(): jnp.einsum('fks,fkc->fsc', gathered, both, preferred_element_type=jnp.flo...  11.3 us
    convert_element_type x1, local copies, waits for them, and re-layouts, per_device(): stacked = stacked.astype(jnp.bfloat16).reshape(F, share, 2, channels)  9.74 us
    ppermute x1, waiting for transfers between devices, with_halo(): lax.ppermute(tail, axis, [(i, (i + 1) % count) for i in range(ends)])  9.4 us
  transfers between devices with their start and end apart: 4, of which 3 were waited for; matrix products, arithmetic and copies ran while one was open for 14% of the time, Pallas kernels for 0%

commit v1 on v0

--- a/solution.py
+++ b/solution.py
@@ -10,6 +10,11 @@
 HALO = 16
 SMOOTH = 64
 K0 = 31
+
+
+def gather_over(array, axis, dim):
+    repeated = jnp.stack([array] * lax.axis_size(axis))
+    return jnp.concatenate(lax.all_to_all(repeated, axis, 0, 0), axis=dim)
 
 
 def turn(bins, steps):
@@ -107,7 +112,7 @@
     picked = lax.all_to_all(picked, "win", 0, 0, tiled=True)
     picked = picked.reshape(groups, bins, 2, windows, share)
     picked = jnp.transpose(picked, (1, 2, 0, 3, 4)).reshape(bins, groups * windows, 2 * share)
-    gathered = lax.all_gather(picked, "chan", axis=0, tiled=True)
+    gathered = gather_over(picked, "chan", 0)
     gathered = gathered.reshape(F, 2 * groups * windows, share)
     own = lax.all_gather(whitened, "win", axis=0, tiled=True)
     own = jnp.transpose(own, (3, 2, 0, 1))

time: 246 us -> 232 us (0.943)
  local copies, waits for them, and re-layouts: 59.7 us -> 49.9 us
  blocking collectives: 34.5 us -> 25.4 us
  starting transfers between devices: 5.06 us -> 13.5 us
  waiting for transfers between devices: 72.8 us -> 69.5 us
    all_gather x1 -> x0, waiting for transfers between devices: 59.2 us -> none  [per_device(): gathered = lax.all_gather(picked, 'chan', axis=0, tiled=True)]
    all_gather x1, waiting for transfers between devices: 0.01 us -> 52.5 us  [per_device(): own = lax.all_gather(whitened, 'win', axis=0, tiled=True)]
    reshape x2 -> x0, local copies, waits for them, and re-layouts: 16.4 us -> none  [the longest x1 15.6 us: per_device(): gathered = gathered.reshape(F, 2 * groups * windows, share)]
    another operation x2 -> x5, local copies, waits for them, and re-layouts: 0.96 us -> 15.1 us  [the longest x1 11 us: per_device(): gathered = gathered.reshape(F, 2 * groups * windows, share)]
    all_to_all x1 -> x0, blocking collectives: 9.1 us -> none  [per_device(): picked = lax.all_to_all(picked, 'win', 0, 0, tiled=True)]
    all_to_all x0 -> x2, starting transfers between devices: none -> 8.42 us  [the longest x1 5.1 us: gather_over(): return jnp.concatenate(lax.all_to_all(repeated, axis, 0, 0), axis=dim)]
    all_gather x1 -> x0, local copies, waits for them, and re-layouts: 7.55 us -> none  [per_device(): gathered = lax.all_gather(picked, 'chan', axis=0, tiled=True)]
    all_to_all x0 -> x2, waiting for transfers between devices: none -> 3.64 us  [the longest x1 3.64 us: per_device(): picked = lax.all_to_all(picked, 'win', 0, 0, tiled=True)]
  transfers between devices with their start and end apart: 4 -> 5, of which waited for: 3 -> 4; matrix products, arithmetic and copies ran while one was open for 14% -> 13% of each run, Pallas kernels for 0% -> 0%
where the time goes in v1:
time: 232 us; the launch traced here: 230 us
  waiting for transfers between devices  69.5 us (30%)
  local copies, waits for them, and re-layouts  49.9 us (22%)
  matrix products  38.1 us (16%)
  blocking collectives  25.4 us (11%)
  other arithmetic  19.5 us (8%)
  between operations  13.7 us (6%)
  starting transfers between devices  13.5 us (6%)
    all_gather x1, waiting for transfers between devices, per_device(): own = lax.all_gather(whitened, 'win', axis=0, tiled=True)  52.5 us
    dot_general x5, matrix products, per_device(): dot = lambda a, b: jnp.dot(a, b, preferred_element_type=jnp.float32)  26.3 us
    all_to_all x1, blocking collectives, per_device(): mixed = lax.all_to_all(split, 'chan', 0, 0, tiled=True)  25.4 us
    concatenate x1, local copies, waits for them, and re-layouts, per_device(): both = jnp.concatenate([left, right], axis=2)  13 us
    another operation x1, local copies, waits for them, and re-layouts, per_device(): gathered = gathered.reshape(F, 2 * groups * windows, share)  11 us
    convert_element_type x1, local copies, waits for them, and re-layouts, per_device(): stacked = stacked.astype(jnp.bfloat16).reshape(F, share, 2, channels)  9.74 us
    dot_general x1, matrix products, per_device(): jnp.einsum('fks,fkc->fsc', gathered, both, preferred_element_type=jnp.flo...  9.32 us
    ppermute x1, waiting for transfers between devices, with_halo(): lax.ppermute(tail, axis, [(i, (i + 1) % count) for i in range(ends)])  9.22 us
  transfers between devices with their start and end apart: 5, of which 4 were waited for; matrix products, arithmetic and copies ran while one was open for 13% of the time, Pallas kernels for 0%

profile of v1, /device:TPU:0, one launch (start us, length us, event | category | flops | bytes accessed | tf_op | source)
XLA Modules:
  0.0 229.7 jit_solution(9359476464815870908)
XLA Ops:
  6.5 0.5 fusion.53
  7.1 1.1 fusion.46
  8.2 4.6 %subtract_convert_fusion = (bf16[120,64,512]{2,1,0:T(8,128)(2,1)S(1)}, bf16[120,64,512]{2,1,0:T(8,128)(2,1)S(1)}) fusion(f32[64,512]{1,0:T(8,128)S(1)} %get-tuple-element.16, f32[120,512]{1,0:T(8,128)S(1)} %get-tuple-element.15, f32[64,512]{1,0:T(8,128)S(1)} %get-tuple-element.14, f32[120,512]{1,0:T(8,128)S(1)} %get-tuple-element.13), kind=kLoop, calls=%fused_computation.2 | loop fusion | flops 35389440 | bytes 16482304 | tf_op jit(solution)/shard_map/convert_element_type | solution.py:33
  12.8 2.2 convolution_bitcast_fusion
  15.1 2.2 convolution_bitcast_fusion.1
  17.4 0.6 copy.29
  18.0 0.9 reshape.172
  18.9 0.2 broadcast_multiply_fusion
  19.1 0.1 fusion.60
  19.2 3.5 %collective-permute-start = (f32[8,16,1024]{2,1,0:T(8,128)S(1)}, f32[8,16,1024]{2,1,0:T(8,128)S(1)}, u32[]{:S(2)}, u32[]{:S(2)}) collective-permute-start(f32[8,16,1024]{2,1,0:T(8,128)S(1)} %get-tuple-element.27), channel_id=1, source_target_pairs={{0,1},{1,2},{2,3},{3,4},{4,5},{5,6},{6,7},{7,8},{8,9},{9,10},{10,1... | collective-permute-start | bytes 1572872 | tf_op jit(solution)/shard_map/ppermute | solution.py:76
  22.8 1.5 collective-permute-start.1
  24.3 0.1 convert_reduce_fusion
  24.5 0.1 select_reduce_fusion
  24.7 9.2 %collective-permute-done = f32[8,16,1024]{2,1,0:T(8,128)S(1)} collective-permute-done((f32[8,16,1024]{2,1,0:T(8,128)S(1)}, f32[8,16,1024]{2,1,0:T(8,128)S(1)}, u32[]{:S(2)}, u32[]{:S(2)}) %collective-permute-start) | collective-permute-done | bytes 524320 | tf_op jit(solution)/shard_map/ppermute | solution.py:76
  33.9 4.1 %collective-permute-done.1 = f32[8,16,1024]{2,1,0:T(8,128)S(1)} collective-permute-done((f32[8,16,1024]{2,1,0:T(8,128)S(1)}, f32[8,16,1024]{2,1,0:T(8,128)S(1)}, u32[]{:S(2)}, u32[]{:S(2)}) %collective-permute-start.1) | collective-permute-done | bytes 524320 | tf_op jit(solution)/shard_map/ppermute | solution.py:77
  38.1 1.2 fusion.14
  39.3 1.3 divide_convert_fusion.1
  40.6 0.5 copy.30
  41.1 0.5 copy.31
  41.6 0.5 maximum_bitcast_fusion
  42.1 2.4 %copy.32 = bf16[32,16,2,8,32]{4,3,2,1,0:T(8,128)(2,1)S(1)} copy(bf16[32,16,2,8,32]{4,1,0,3,2:T(8,128)(2,1)S(1)} %maximum_bitcast_fusion) | data formatting | bytes 1048576 | tf_op jit(solution)/shard_map/transpose | solution.py:102
  44.5 1.5 reshape.173
  46.0 25.4 %all_to_all.15 = bf16[32,32,256]{2,1,0:T(8,128)(2,1)S(1)} all-to-all(bf16[32,32,256]{2,1,0:T(8,128)(2,1)S(1)} %reshape.173), channel_id=1, replica_groups=mesh['win'=4,'chan'=32] {'chan'}, dimensions={0} | all-to-all | bytes 1048576 | tf_op jit(solution)/shard_map/all_to_all | solution.py:103
  71.4 0.9 reshape.174
  72.3 0.8 copy.33
  73.1 1.2 convolution_convert_fusion.1
  74.3 3.3 %all-to-all-start.1 = ((bf16[4,256,64]{1,2,0:T(8,128)(2,1)}), bf16[4,256,64]{1,2,0:T(8,128)(2,1)S(1)}, u32[]{:S(2)}, u32[]{:S(2)}) async-start(bf16[4,256,64]{1,2,0:T(8,128)(2,1)} %bitcast.16), calls=%async_computation.1 | async-start | bytes 262144 | tf_op jit(solution)/shard_map/all_to_all | solution.py:112
  77.7 0.8 pad_maximum_fusion.1
  78.5 3.6 %all-to-all-done.1 = bf16[4,256,64]{1,2,0:T(8,128)(2,1)S(1)} async-done(((bf16[4,256,64]{1,2,0:T(8,128)(2,1)}), bf16[4,256,64]{1,2,0:T(8,128)(2,1)S(1)}, u32[]{:S(2)}, u32[]{:S(2)}) %all-to-all-start.1) | async-done | bytes 131104 | tf_op jit(solution)/shard_map/all_to_all | solution.py:112
  82.2 0.2 copy.34
  82.4 0.1 stack_reshape.2
  82.6 3.0 %stack.36 = bf16[32,16,32,128]{3,2,1,0:T(8,128)(2,1)} broadcast(bf16[16,32,128]{2,1,0:T(8,128)(2,1)S(1)} %stack_reshape.2), dimensions={1,2,3} | broadcast | bytes 4325376 | tf_op jit(solution)/shard_map/stack | solution.py:16
  85.5 5.1 %all-to-all-start.2 = ((bf16[32,16,32,128]{3,2,1,0:T(8,128)(2,1)}), bf16[32,16,32,128]{3,2,1,0:T(8,128)(2,1)}, u32[]{:S(2)}, u32[]{:S(2)}) async-start(bf16[32,16,32,128]{3,2,1,0:T(8,128)(2,1)} %stack.36), calls=%async_computation.2 | async-start | bytes 8388608 | tf_op jit(solution)/shard_map/all_to_all | solution.py:17
  90.6 1.1 fusion.34
  91.8 1.1 fusion.38
  92.9 5.5 %negate_convert_fusion.1 = (bf16[512,16,128]{2,1,0:T(8,128)(2,1)S(1)}, bf16[512,16,128]{2,1,0:T(8,128)(2,1)}) fusion(f32[512,128]{1,0:T(8,128)S(1)} %get-tuple-element.20, f32[512,16]{1,0:T(8,128)S(1)} %get-tuple-element.19, f32[512,128]{1,0:T(8,128)S(1)} %get-tuple-element.18, f32[512,16]{1,0:T(8,128)S(1)} %get-tuple-element.17), kind=kLoop, calls=%fused_computation.5 | loop fusion | flops 9437184 | bytes 4784128 | tf_op jit(solution)/shard_map/convert_element_type | solution.py:46
  98.4 52.5 %all-gather.2.cloned.1.call-done = bf16[32,32,2,512]{3,1,0,2:T(8,128)(2,1)} async-done(((bf16[8,32,2,512]{3,1,0,2:T(8,128)(2,1)}), bf16[32,32,2,512]{3,1,0,2:T(8,128)(2,1)}) %all-gather.2.cloned.1.call-update) | async-done | bytes 2097168 | tf_op jit(solution)/shard_map/all_gather | solution.py:117
  151.0 1.3 fusion.59
  152.2 1.8 slice_bitcast_fusion.5
  154.0 2.2 maximum_maximum_fusion
  156.2 13.0 %copy.37 = bf16[512,64,64]{2,1,0:T(8,128)(2,1)} copy(bf16[512,64,64]{0,2,1:T(8,128)(2,1)} %maximum_maximum_fusion) | data formatting | bytes 8388608 | tf_op jit(solution)/shard_map/concatenate | solution.py:122
  169.2 11.0 %reshape_reshape.3 = bf16[512,64,64]{2,1,0:T(8,128)(2,1)} reshape(bf16[32,16,32,128]{3,2,1,0:T(8,128)(2,1)} %all-to-all-done.2) | data formatting | bytes 8388608 | tf_op jit(solution)/shard_map/reshape;reshape | solution.py:116
  180.3 9.3 %convolution_convert_fusion = bf16[512,64,64]{2,1,0:T(8,128)(2,1)} fusion(bf16[512,64,64]{2,1,0:T(8,128)(2,1)} %reshape_reshape.3, bf16[512,64,64]{2,1,0:T(8,128)(2,1)} %copy.37), kind=kOutput, calls=%fused_computation.3 | convolution fusion | flops 270532608 | bytes 12582912 | tf_op jit(solution)/shard_map/fks,fkc->fsc/dot_general | solution.py:123
  189.6 9.7 %copy.38 = bf16[512,64,64]{0,2,1:T(8,128)(2,1)} copy(bf16[512,64,64]{2,1,0:T(8,128)(2,1)} %convolution_convert_fusion) | data formatting | bytes 8388608 | tf_op jit(solution)/shard_map/convert_element_type | solution.py:124
  199.3 2.7 %copy.39 = bf16[64,32,2,512]{3,1,0,2:T(8,128)(2,1)S(1)} copy(bf16[64,32,2,512]{3,1,2,0:T(8,128)(2,1)} %bitcast.74) | data formatting | bytes 8388608 | tf_op jit(solution)/shard_map/transpose | solution.py:125
  202.0 0.2 copy-done
  202.2 8.6 %fusion.2 = f32[2048,2048]{1,0:T(8,128)} fusion(bf16[64,8,16,128]{3,2,1,0:T(8,128)(2,1)S(1)} %bitcast.85, bf16[2048,2,512]{2,0,1:T(8,128)(2,1)S(1)} %bitcast.75), kind=kOutput, calls=%fused_computation.9 | convolution fusion | flops 4294967296 | bytes 20971520 | tf_op jit(solution)/shard_map/dot_general | solution.py:90
  210.8 12.0 %add_multiply_fusion = f32[2048,2048]{1,0:T(8,128)} fusion(f32[2048,2048]{1,0:T(8,128)} %fusion.2, bf16[64,8,16,128]{3,2,1,0:T(8,128)(2,1)S(1)} %bitcast.77, bf16[2048,2,512]{2,0,1:T(8,128)(2,1)S(1)} %bitcast.76), kind=kOutput, calls=%fused_computation | convolution fusion | flops 4303355904 | bytes 37748736 | tf_op jit(solution)/shard_map/dot_general | solution.py:90
  (25 shorter events, 0.4 us)
Async XLA Ops:
  8.2 4.7 %copy-start.4 = (bf16[8,32,7680]{2,1,0:T(8,128)(2,1)S(1)}, bf16[8,32,7680]{2,1,0:T(8,128)(2,1)}, u32[]{:S(2)}) copy-start(bf16[8,32,7680]{2,1,0:T(8,128)(2,1)} %param.4) | copy-start | bytes 11796484
  17.3 1.6 copy-start.6
  17.4 7.0 %copy-start.3 = (bf16[32]{0:T(256)(128)(2,1)S(1)}, bf16[32]{0:T(256)(128)(2,1)}, u32[]{:S(2)}) copy-start(bf16[32]{0:T(256)(128)(2,1)} %param.5) | copy-start | bytes 196
  19.2 14.7 %collective-permute-start = (f32[8,16,1024]{2,1,0:T(8,128)S(1)}, f32[8,16,1024]{2,1,0:T(8,128)S(1)}, u32[]{:S(2)}, u32[]{:S(2)}) collective-permute-start(f32[8,16,1024]{2,1,0:T(8,128)S(1)} %get-tuple-element.27), channel_id=1, source_target_pairs={{0,1},{1,2},{2,3},{3,4},{4,5},{5,6},{6,7},{7,8},{8,9},{9,10},{10,1... | collective-permute-start | bytes 1572872 | tf_op jit(solution)/shard_map/ppermute | solution.py:76
  22.8 15.3 %collective-permute-start.1 = (f32[8,16,1024]{2,1,0:T(8,128)S(1)}, f32[8,16,1024]{2,1,0:T(8,128)S(1)}, u32[]{:S(2)}, u32[]{:S(2)}) collective-permute-start(f32[8,16,1024]{2,1,0:T(8,128)S(1)} %get-tuple-element.28), channel_id=1, source_target_pairs={{1,0},{2,1},{3,2},{4,3},{5,4},{6,5},{7,6},{8,7},{9,8},{10,9},{11,1... | collective-permute-start | bytes 1572872 | tf_op jit(solution)/shard_map/ppermute | solution.py:77
  40.6 1.5 copy-start.1
  44.5 28.6 %copy-start.5 = (s32[256]{0:T(256)S(1)}, s32[256]{0:T(256)}, u32[]{:S(2)}) copy-start(s32[256]{0:T(256)} %param.7) | copy-start | bytes 3076
  71.4 6.3 %copy-start.2 = (bf16[8,32,512]{2,1,0:T(8,128)(2,1)S(1)}, bf16[8,32,512]{2,1,0:T(8,128)(2,1)}, u32[]{:S(2)}) copy-start(bf16[8,32,512]{2,1,0:T(8,128)(2,1)} %copy-done.1) | copy-start | bytes 786436
  74.3 7.9 %all-to-all-start.1 = ((bf16[4,256,64]{1,2,0:T(8,128)(2,1)}), bf16[4,256,64]{1,2,0:T(8,128)(2,1)S(1)}, u32[]{:S(2)}, u32[]{:S(2)}) async-start(bf16[4,256,64]{1,2,0:T(8,128)(2,1)} %bitcast.16), calls=%async_computation.1 | async-start | bytes 262144 | tf_op jit(solution)/shard_map/all_to_all | solution.py:112
  77.6 73.3 %all-gather.2.cloned.1.call-start = ((), (), s32[]{:S(2)}) async-start(), calls=%async_computation.3 | async-start | bytes 2621440 | tf_op jit(solution)/shard_map/all_gather | solution.py:117
  85.5 83.7 %all-to-all-start.2 = ((bf16[32,16,32,128]{3,2,1,0:T(8,128)(2,1)}), bf16[32,16,32,128]{3,2,1,0:T(8,128)(2,1)}, u32[]{:S(2)}, u32[]{:S(2)}) async-start(bf16[32,16,32,128]{3,2,1,0:T(8,128)(2,1)} %stack.36), calls=%async_computation.2 | async-start | bytes 8388608 | tf_op jit(solution)/shard_map/all_to_all | solution.py:17
  199.3 2.9 %copy-start = (bf16[512,16,128]{2,1,0:T(8,128)(2,1)S(1)}, bf16[512,16,128]{2,1,0:T(8,128)(2,1)}, u32[]{:S(2)}) copy-start(bf16[512,16,128]{2,1,0:T(8,128)(2,1)} %get-tuple-element.26) | copy-start | bytes 6291460
Sparse Core Ops, SparseCore 0:
  80.1 70.8 all-gather.1
